TPU v7x, 256 devices: a whole 4x4x8 slice. The times are simulated.
256 devices in a mesh: buf: 32 (over x, y, core), lat: 8 (over z).
Axes of the slice: x: 4, y: 4, z: 8, core: 2. Of those that a mesh axis runs over, the one named last changes fastest.
Arguments:
- buffer: bfloat16 [8192, 4096], P('buf'), may hold values from -6 to 6
- sample_rows: int32 [8192], P('lat'), may hold values from 0 to 8191, as said below
- window: bfloat16 [24576, 4096], P('buf'), may hold values from -6 to 6
- enc_scale: float32 [8192], P('lat'), may hold values from 0.5 to 2
- dec_bias: float32 [4096], replicated, may hold values from -3 to 3
Outputs:
- recon: bfloat16 [24576, 4096], P('buf', 'lat')
Inputs may be any that keep to these rules, and one draw needn't show every extreme that they name: `sample_rows`: entry k names the buffer row sampled for reseeded latent k; shard s of the buffer holds rows s * 256 to (s + 1) * 256 - 1. In each aligned block of 32 entries at most 2 name rows of one shard, and in every block some shard gives exactly 2. In each owner's 1024 entries at most 64 name rows of one shard, and some shard gives exactly 64.
All inputs are finite; a program needn't handle non-finite values.
Results may differ from a plain program's by a relative error of at most 0.018.
Values may be sent and summed in bfloat16 or wider, within the bound.
A program may use at most 128 MiB of HBM per device.

v0:
```python
import jax
import jax.numpy as jnp
from jax import lax
from jax.sharding import PartitionSpec as P


def unit_rows(picked_rows):
    values = picked_rows.astype(jnp.float32)
    squares = jnp.sum(values * values, axis=1, keepdims=True)
    return (values * lax.rsqrt(squares + 1e-06)).astype(jnp.bfloat16)


def encode_block(centered, unit_block, scale_block):
    scores = lax.dot_general(
        centered, unit_block, (((1,), (1,)), ((), ())), preferred_element_type=jnp.float32
    )
    return jnp.maximum(scores * scale_block[None, :], 0.0).astype(jnp.bfloat16)


def pick_units(buffer, pick_index):
    picked = jnp.take(buffer, jnp.maximum(pick_index, 0), axis=0)
    picked = jnp.where((pick_index >= 0)[:, None], picked, jnp.zeros_like(picked))
    return unit_rows(picked)


def on_device(buffer, sample_rows, window, enc_scale, dec_bias):
    shard_count = lax.axis_size("buf")
    shard_index = lax.axis_index("buf")
    owner_count = sample_rows.shape[0]
    slot_count = owner_count // shard_count
    shard_rows = buffer.shape[0]
    capacity = 2 + (slot_count - 1) // shard_count
    source = sample_rows // shard_rows
    offset = sample_rows - source * shard_rows
    centered = (window.astype(jnp.float32) - dec_bias[None, :]).astype(jnp.bfloat16)
    positions = jnp.arange(owner_count, dtype=jnp.int32)
    own_capacity = shard_count * capacity
    matching = source[:, None] == source[None, :]
    earlier = positions[:, None] < positions[None, :]
    owner_rank = jnp.sum((matching & earlier).astype(jnp.int32), axis=0)
    room_iota = jnp.arange(own_capacity, dtype=jnp.int32)
    chosen = (source == shard_index)[:, None] & (owner_rank[:, None] == room_iota[None, :])
    pick_index = jnp.sum(jnp.where(chosen, offset[:, None] + 1, 0), axis=0) - 1
    packed = pick_units(buffer, pick_index)
    collected = lax.all_gather(packed, "buf", axis=0, tiled=True)
    all_units = jnp.take(collected, source * own_capacity + owner_rank, axis=0)
    active_all = encode_block(centered, all_units, enc_scale)
    partial_value = jnp.dot(active_all, all_units, preferred_element_type=jnp.float32)
    rounded = partial_value.astype(jnp.bfloat16).astype(jnp.float32)
    summed = lax.psum_scatter(
        rounded.astype(jnp.bfloat16), "lat", scatter_dimension=1, tiled=True
    ).astype(jnp.float32)
    feature_count = summed.shape[1]
    bias_part = lax.dynamic_slice_in_dim(
        dec_bias, lax.axis_index("lat") * feature_count, feature_count
    )
    return (summed + bias_part[None, :]).astype(jnp.bfloat16)


def solution(mesh):
    in_specs = (P("buf", None), P("lat"), P("buf", None), P("lat"), P())
    out_specs = P("buf", "lat")
    return jax.shard_map(
        on_device, mesh=mesh, in_specs=in_specs, out_specs=out_specs, check_vma=False
    )
```

profile of v0, /device:TPU:1, one launch (start us, length us, event | category | flops | bytes accessed | tf_op | source)
XLA Modules:
  0.0 220.5 jit_solution(11854953599494018754)
XLA Ops:
  6.5 0.0 copy-start
  6.5 0.0 all-gather.2.cloned.1.call-start
  6.5 0.8 add_select_fusion
  7.4 0.4 convert_reduce_fusion
  7.8 0.7 broadcast_clamp_fusion
  8.5 0.7 compare_and_fusion
  9.2 0.2 select_reduce_fusion
  9.4 0.0 copy-done
  9.4 0.9 gather_fusion
  10.3 0.3 fusion.3
  10.6 1.0 fusion.4
  11.7 0.0 all-gather.2.cloned.1.call-update
  11.7 0.0 reduce-scatter.2.cloned.1.call-start
  11.7 81.8 %all-gather.2.cloned.1.call-done = bf16[2048,4096]{1,0:T(8,128)(2,1)} async-done(((bf16[64,4096]{1,0:T(8,128)(2,1)}), bf16[2048,4096]{1,0:T(8,128)(2,1)}) %all-gather.2.cloned.1.call-update) | async-done | bytes 16777232 | tf_op jit(solution)/shard_map/all_gather | solution.py:45
  93.6 23.0 %gather_fusion.1 = bf16[1024,4096]{1,0:T(8,128)(2,1)} fusion(bf16[2048,4096]{1,0:T(8,128)(2,1)} %all-gather.2.cloned.1.call-done, s32[1024]{0:T(1024)S(1)} %get-tuple-element.7), kind=kCustom, calls=%fused_computation.1 | custom fusion | bytes 16781312 | tf_op jit(solution)/shard_map/jit(_take)/gather | solution.py:46
  116.6 0.0 copy-done.2
  116.6 0.0 copy-done.3
  116.6 11.6 %maximum_convert_fusion = bf16[768,1024]{1,0:T(8,128)(2,1)S(1)} fusion(bf16[1024,4096]{1,0:T(8,128)(2,1)} %gather_fusion.1, pred[1024]{0:T(1024)(128)(4,1)S(1)} %get-tuple-element.5, bf16[768,4096]{1,0:T(8,128)(2,1)} %param.7, f32[4096]{0:T(1024)S(1)} %copy-done.2, f32[1024]{0:T(1024)S(1)} %copy-done.3), kind=kOutput, calls=%fused_computation.10 | convolution fusion | flops 6458441728 | bytes 16274432 | tf_op jit(solution)/shard_map/dot_general | solution.py:14
  128.3 0.0 copy-done.1
  128.3 8.8 %convolution_convert_fusion = bf16[768,4096]{1,0:T(8,128)(2,1)} fusion(bf16[768,1024]{1,0:T(8,128)(2,1)S(1)} %maximum_convert_fusion, bf16[1024,4096]{1,0:T(8,128)(2,1)S(1)} %copy-done.1, pred[1024]{0:T(1024)(128)(4,1)S(1)} %get-tuple-element.5), kind=kOutput, calls=%fused_computation.4 | convolution fusion | flops 6449790976 | bytes 16253952 | tf_op jit(solution)/shard_map/dot_general | solution.py:48
  137.1 0.0 reduce-scatter.2.cloned.1.call-update
  137.1 0.1 dynamic_slice.3
  137.2 74.4 %reduce-scatter.2.cloned.1.call-done = bf16[768,512]{1,0:T(8,128)(2,1)} async-done(((bf16[768,4096]{1,0:T(8,128)(2,1)}), bf16[768,512]{1,0:T(8,128)(2,1)}) %reduce-scatter.2.cloned.1.call-update) | async-done | bytes 786448 | tf_op jit(solution)/shard_map/reduce_scatter | solution.py:50
  211.5 2.2 add_convert_fusion
  (7 shorter events, 0.0 us)
Async XLA Ops:
  6.5 2.9 %copy-start = (bf16[256,4096]{1,0:T(8,128)(2,1)S(1)}, bf16[256,4096]{1,0:T(8,128)(2,1)}, u32[]{:S(2)}) copy-start(bf16[256,4096]{1,0:T(8,128)(2,1)} %param.5) | copy-start | bytes 6291460
  6.5 87.0 %all-gather.2.cloned.1.call-start = ((), (), s32[]{:S(2)}) async-start(), calls=%async_computation.1 | async-start | bytes 17301504 | tf_op jit(solution)/shard_map/all_gather | solution.py:45
  11.7 199.9 %reduce-scatter.2.cloned.1.call-start = ((), (), s32[]{:S(2)}) async-start(), calls=%async_computation.2 | async-start | bytes 7077888 | tf_op jit(solution)/shard_map/reduce_scatter | solution.py:50
  93.6 23.0 %copy-start.2 = (f32[4096]{0:T(1024)S(1)}, f32[4096]{0:T(1024)}, u32[]{:S(2)}) copy-start(f32[4096]{0:T(1024)} %param.9) | copy-start | bytes 49156
  93.6 23.0 %copy-start.3 = (f32[1024]{0:T(1024)S(1)}, f32[1024]{0:T(1024)}, u32[]{:S(2)}) copy-start(f32[1024]{0:T(1024)} %param.8) | copy-start | bytes 12292
  116.6 11.7 %copy-start.1 = (bf16[1024,4096]{1,0:T(8,128)(2,1)S(1)}, bf16[1024,4096]{1,0:T(8,128)(2,1)}, u32[]{:S(2)}) copy-start(bf16[1024,4096]{1,0:T(8,128)(2,1)} %gather_fusion.1) | copy-start | bytes 25165828
Sparse Core Ops, SparseCore 0:
  11.8 81.7 all-gather.1
  137.2 74.2 reduce-scatter.1
where the time goes:
time: 221 us
  waiting for transfers between devices  156 us (71%)
  local copies, waits for them, and re-layouts  24 us (11%)
  matrix products  20.4 us (9%)
  between operations  13.5 us (6%)
  other arithmetic  6.37 us (3%)
    all_gather x1, waiting for transfers between devices, on_device(): collected = lax.all_gather(packed, 'buf', axis=0, tiled=True)  81.8 us
    reduce_scatter x1, waiting for transfers between devices, on_device(): lax.psum_scatter(rounded.astype(jnp.bfloat16), 'lat', scatter_dimension=1...  74.4 us
    gather x1, local copies, waits for them, and re-layouts, on_device(): all_units = jnp.take(collected, source * own_capacity + owner_rank, axis=0)  23 us
    dot_general x1, matrix products, encode_block(): lax.dot_general(centered, unit_block, (((1,), (1,)), ((), ())), preferred...  11.6 us
    dot_general x1, matrix products, on_device(): jnp.dot(active_all, all_units, preferred_element_type=jnp.float32)  8.79 us
  transfers between devices with their start and end apart: 2, of which 2 were waited for; matrix products, arithmetic and copies ran while one was open for 0% of the time, Pallas kernels for 0%

commit v1 on v0

--- a/solution.py
+++ b/solution.py
@@ -2,6 +2,7 @@
 import jax.numpy as jnp
 from jax import lax
 from jax.sharding import PartitionSpec as P
+from jax.lax import axis_index, axis_size, ppermute
 
 
 def unit_rows(picked_rows):
@@ -42,7 +43,22 @@
     chosen = (source == shard_index)[:, None] & (owner_rank[:, None] == room_iota[None, :])
     pick_index = jnp.sum(jnp.where(chosen, offset[:, None] + 1, 0), axis=0) - 1
     packed = pick_units(buffer, pick_index)
-    collected = lax.all_gather(packed, "buf", axis=0, tiled=True)
+
+    def members_all_prepare(inp, mesh_name="buf"):
+        spare = axis_size(mesh_name)
+        found_now = axis_index(mesh_name)
+        outcome_arr, far_arr = (spare, found_now)
+        now, near = (inp, 1)
+        while near < outcome_arr:
+            part_next = tuple(((j0, j0 ^ near) for j0 in range(outcome_arr)))
+            carry = ppermute(now, axis_name=mesh_name, perm=part_next)
+            long_array = jnp.concatenate([now, carry], axis=0)
+            local_now = jnp.concatenate([carry, now], axis=0)
+            now = jnp.where(far_arr & near == 0, long_array, local_now)
+            near = 2 * near
+        return now
+
+    collected = members_all_prepare(packed)
     all_units = jnp.take(collected, source * own_capacity + owner_rank, axis=0)
     active_all = encode_block(centered, all_units, enc_scale)
     partial_value = jnp.dot(active_all, all_units, preferred_element_type=jnp.float32)

time: 221 us -> 529 us (2.39)
  waiting for transfers between devices: 156 us -> 422 us
  other arithmetic: 6.37 us -> 43.1 us
  starting transfers between devices: 0.04 us -> 5.7 us
    ppermute x0 -> x5, waiting for transfers between devices: none -> 342 us  [members_all_prepare(): carry = ppermute(now, axis_name=mesh_name, perm=part_next)]
    all_gather x1 -> x0, waiting for transfers between devices: 81.8 us -> none  [on_device(): collected = lax.all_gather(packed, 'buf', axis=0, tiled=True)]
    select_n x0 -> x5, other arithmetic: none -> 37.5 us  [members_all_prepare(): now = jnp.where(far_arr & near == 0, long_array, local_now)]
    ppermute x0 -> x5, starting transfers between devices: none -> 5.7 us  [members_all_prepare(): carry = ppermute(now, axis_name=mesh_name, perm=part_next)]
    reduce_scatter x1, waiting for transfers between devices: 74.4 us -> 79.8 us  [on_device(): lax.psum_scatter(rounded.astype(jnp.bfloat16), 'lat', scatter_dimension=1...]
  transfers between devices with their start and end apart: 2 -> 6, of which waited for: 2 -> 6; matrix products, arithmetic and copies ran while one was open for 0% -> 0% of each run, Pallas kernels for 0% -> 0%
where the time goes in v1:
time: 529 us
  waiting for transfers between devices  422 us (80%)
  other arithmetic  43.1 us (8%)
  local copies, waits for them, and re-layouts  24 us (5%)
  matrix products  20.6 us (4%)
  between operations  13.5 us (3%)
  starting transfers between devices  5.7 us (1%)
    ppermute x5, waiting for transfers between devices, members_all_prepare(): carry = ppermute(now, axis_name=mesh_name, perm=part_next)  342 us
    reduce_scatter x1, waiting for transfers between devices, on_device(): lax.psum_scatter(rounded.astype(jnp.bfloat16), 'lat', scatter_dimension=1...  79.8 us
    select_n x5, other arithmetic, members_all_prepare(): now = jnp.where(far_arr & near == 0, long_array, local_now)  37.5 us
    gather x1, local copies, waits for them, and re-layouts, on_device(): all_units = jnp.take(collected, source * own_capacity + owner_rank, axis=0)  23 us
    dot_general x1, matrix products, encode_block(): lax.dot_general(centered, unit_block, (((1,), (1,)), ((), ())), preferred...  11.6 us
  transfers between devices with their start and end apart: 6, of which 6 were waited for; matrix products, arithmetic and copies ran while one was open for 0% of the time, Pallas kernels for 0%

profile of v1, /device:TPU:1, one launch (start us, length us, event | category | flops | bytes accessed | tf_op | source)
XLA Modules:
  0.0 528.9 jit_solution(11258948766792162898)
XLA Ops:
  6.5 0.8 add_select_fusion
  7.4 0.4 convert_reduce_fusion
  7.8 0.7 broadcast_clamp_fusion
  8.5 0.7 compare_and_fusion
  9.4 0.9 gather_fusion
  10.3 0.3 fusion.3
  10.6 0.2 fusion.4
  10.9 3.3 collective-permute-start
  14.2 1.5 collective-permute-done
  16.1 24.5 %collective-permute-done.1 = bf16[128,4096]{1,0:T(8,128)(2,1)} collective-permute-done((bf16[128,4096]{1,0:T(8,128)(2,1)S(1)}, bf16[128,4096]{1,0:T(8,128)(2,1)}, u32[]{:S(2)}, u32[]{:S(2)}) %collective-permute-start.1) | collective-permute-done | bytes 1048608 | tf_op jit(solution)/shard_map/ppermute | solution.py:54
  40.5 2.3 maximum_select_fusion.3
  42.8 1.3 collective-permute-start.2
  44.1 46.4 %collective-permute-done.2 = bf16[256,4096]{1,0:T(8,128)(2,1)} collective-permute-done((bf16[256,4096]{1,0:T(8,128)(2,1)S(1)}, bf16[256,4096]{1,0:T(8,128)(2,1)}, u32[]{:S(2)}, u32[]{:S(2)}) %collective-permute-start.2) | collective-permute-done | bytes 2097184 | tf_op jit(solution)/shard_map/ppermute | solution.py:54
  90.4 5.1 maximum_select_fusion.2
  95.6 90.3 %collective-permute-done.3 = bf16[512,4096]{1,0:T(8,128)(2,1)} collective-permute-done((bf16[512,4096]{1,0:T(8,128)(2,1)}, bf16[512,4096]{1,0:T(8,128)(2,1)}, u32[]{:S(2)}, u32[]{:S(2)}) %collective-permute-start.3) | collective-permute-done | bytes 4194336 | tf_op jit(solution)/shard_map/ppermute | solution.py:54
  185.8 11.1 %maximum_select_fusion.1 = bf16[1024,4096]{1,0:T(8,128)(2,1)} fusion(bf16[512,4096]{1,0:T(8,128)(2,1)} %collective-permute-done.3, bf16[512,4096]{1,0:T(8,128)(2,1)} %maximum_select_fusion.2, pred[]{:T(512)S(6)} %eq.51), kind=kLoop, calls=%fused_computation.4 | loop fusion | flops 37748736 | bytes 16777216 | tf_op jit(solution)/shard_map/jit(_where)/select_n | solution.py:57
  196.9 1.0 collective-permute-start.4
  197.9 179.7 %collective-permute-done.4 = bf16[1024,4096]{1,0:T(8,128)(2,1)} collective-permute-done((bf16[1024,4096]{1,0:T(8,128)(2,1)}, bf16[1024,4096]{1,0:T(8,128)(2,1)}, u32[]{:S(2)}, u32[]{:S(2)}) %collective-permute-start.4) | collective-permute-done | bytes 8388640 | tf_op jit(solution)/shard_map/ppermute | solution.py:54
  377.6 18.8 %maximum_select_fusion = bf16[2048,4096]{1,0:T(8,128)(2,1)} fusion(bf16[1024,4096]{1,0:T(8,128)(2,1)} %collective-permute-done.4, bf16[1024,4096]{1,0:T(8,128)(2,1)} %maximum_select_fusion.1, pred[]{:T(512)S(6)} %eq.50), kind=kLoop, calls=%fused_computation.2 | loop fusion | flops 75497472 | bytes 33554432 | tf_op jit(solution)/shard_map/jit(_where)/select_n | solution.py:57
  396.4 23.0 %gather_fusion.1 = bf16[1024,4096]{1,0:T(8,128)(2,1)} fusion(bf16[2048,4096]{1,0:T(8,128)(2,1)} %maximum_select_fusion, s32[1024]{0:T(1024)S(1)} %get-tuple-element.7), kind=kCustom, calls=%fused_computation.1 | custom fusion | bytes 16781312 | tf_op jit(solution)/shard_map/jit(_take)/gather | solution.py:62
  419.5 11.6 %maximum_convert_fusion = bf16[768,1024]{1,0:T(8,128)(2,1)S(1)} fusion(bf16[1024,4096]{1,0:T(8,128)(2,1)} %gather_fusion.1, pred[1024]{0:T(1024)(128)(4,1)S(1)} %get-tuple-element.5, bf16[768,4096]{1,0:T(8,128)(2,1)} %param.7, f32[4096]{0:T(1024)S(1)} %copy-done.3, f32[1024]{0:T(1024)S(1)} %copy-done.4), kind=kOutput, calls=%fused_computation.13 | convolution fusion | flops 6458441728 | bytes 16274432 | tf_op jit(solution)/shard_map/dot_general | solution.py:15
  431.1 8.9 %convolution_convert_fusion = bf16[768,4096]{1,0:T(8,128)(2,1)} fusion(bf16[768,1024]{1,0:T(8,128)(2,1)S(1)} %maximum_convert_fusion, bf16[1024,4096]{1,0:T(8,128)(2,1)S(1)} %copy-done.2, pred[1024]{0:T(1024)(128)(4,1)S(1)} %get-tuple-element.5), kind=kOutput, calls=%fused_computation.6 | convolution fusion | flops 6449790976 | bytes 16253952 | tf_op jit(solution)/shard_map/dot_general | solution.py:64
  440.1 79.8 %reduce-scatter.2.cloned.1.call-done = bf16[768,512]{1,0:T(8,128)(2,1)} async-done(((bf16[768,4096]{1,0:T(8,128)(2,1)}), bf16[768,512]{1,0:T(8,128)(2,1)}) %reduce-scatter.2.cloned.1.call-update) | async-done | bytes 786448 | tf_op jit(solution)/shard_map/reduce_scatter | solution.py:66
  519.9 2.2 add_convert_fusion
  (21 shorter events, 0.6 us)
Async XLA Ops:
  6.5 2.9 copy-start
  6.5 513.4 %reduce-scatter.2.cloned.1.call-start = ((), (), s32[]{:S(2)}) async-start(), calls=%async_computation.1 | async-start | bytes 7077888 | tf_op jit(solution)/shard_map/reduce_scatter | solution.py:66
  10.9 4.9 collective-permute-start
  16.0 24.6 %collective-permute-start.1 = (bf16[128,4096]{1,0:T(8,128)(2,1)S(1)}, bf16[128,4096]{1,0:T(8,128)(2,1)}, u32[]{:S(2)}, u32[]{:S(2)}) collective-permute-start(bf16[128,4096]{1,0:T(8,128)(2,1)S(1)} %maximum_select_fusion.4), channel_id=1, source_target_pairs={{0,16},{8,24},{16,0},{24,8},{32,48},{40,56},{48,32},{56,40},{64,80... | collective-permute-start | bytes 3145736 | tf_op jit(solution)/shard_map/ppermute | solution.py:54
  42.8 47.6 %collective-permute-start.2 = (bf16[256,4096]{1,0:T(8,128)(2,1)S(1)}, bf16[256,4096]{1,0:T(8,128)(2,1)}, u32[]{:S(2)}, u32[]{:S(2)}) collective-permute-start(bf16[256,4096]{1,0:T(8,128)(2,1)S(1)} %maximum_select_fusion.3), channel_id=1, source_target_pairs={{0,32},{8,40},{16,48},{24,56},{32,0},{40,8},{48,16},{56,24},{64,96... | collective-permute-start | bytes 6291464 | tf_op jit(solution)/shard_map/ppermute | solution.py:54
  95.6 90.3 %collective-permute-start.3 = (bf16[512,4096]{1,0:T(8,128)(2,1)}, bf16[512,4096]{1,0:T(8,128)(2,1)}, u32[]{:S(2)}, u32[]{:S(2)}) collective-permute-start(bf16[512,4096]{1,0:T(8,128)(2,1)} %maximum_select_fusion.2), channel_id=1, source_target_pairs={{0,64},{8,72},{16,80},{24,88},{32,96},{40,104},{48,112},{56,120},{... | collective-permute-start | bytes 12582920 | tf_op jit(solution)/shard_map/ppermute | solution.py:54
  196.9 180.7 %collective-permute-start.4 = (bf16[1024,4096]{1,0:T(8,128)(2,1)}, bf16[1024,4096]{1,0:T(8,128)(2,1)}, u32[]{:S(2)}, u32[]{:S(2)}) collective-permute-start(bf16[1024,4096]{1,0:T(8,128)(2,1)} %maximum_select_fusion.1), channel_id=1, source_target_pairs={{0,128},{8,136},{16,144},{24,152},{32,160},{40,168},{48,176},{56,1... | collective-permute-start | bytes 25165832 | tf_op jit(solution)/shard_map/ppermute | solution.py:54
  396.4 23.0 %copy-start.3 = (f32[4096]{0:T(1024)S(1)}, f32[4096]{0:T(1024)}, u32[]{:S(2)}) copy-start(f32[4096]{0:T(1024)} %param.9) | copy-start | bytes 49156
  396.4 23.0 %copy-start.4 = (f32[1024]{0:T(1024)S(1)}, f32[1024]{0:T(1024)}, u32[]{:S(2)}) copy-start(f32[1024]{0:T(1024)} %param.8) | copy-start | bytes 12292
  419.4 11.7 %copy-start.2 = (bf16[1024,4096]{1,0:T(8,128)(2,1)S(1)}, bf16[1024,4096]{1,0:T(8,128)(2,1)}, u32[]{:S(2)}) copy-start(bf16[1024,4096]{1,0:T(8,128)(2,1)} %gather_fusion.1) | copy-start | bytes 25165828
  431.1 90.9 %copy-start.1 = (bf16[256,4096]{1,0:T(8,128)(2,1)S(1)}, bf16[256,4096]{1,0:T(8,128)(2,1)}, u32[]{:S(2)}) copy-start(bf16[256,4096]{1,0:T(8,128)(2,1)} %param.5) | copy-start | bytes 6291460
Sparse Core Ops, SparseCore 0:
  440.2 79.6 reduce-scatter.1
